TPU v7x, 32 devices: a whole 2x2x4 slice. The times are simulated.
32 devices in a mesh: row: 8 (over y, x, core), col: 4 (over z).
Axes of the slice: x: 2, y: 2, z: 4, core: 2. Of those that a mesh axis runs over, the one named last changes fastest.
Arguments:
- design: bfloat16 [512, 90112], P(('row', 'col')), may hold values from -6 to 6
- arc_partials: float32 [32, 6, 16], P(('row', 'col')), may hold values from -6 to 6
- arc_id: int32 [32], P(('row', 'col')), may hold values from 0 to 7
- arc_weight: float32 [8], replicated, may hold values from 0.25 to 4
Outputs:
- normal_slab: float32 [90112, 2048], P('row', 'col')
All inputs are finite; a program needn't handle non-finite values.
Results may differ from a plain program's by a relative error of at most 0.0003.
The roundings to bfloat16 on the way count: a program that leaves them out, or rounds other values in their place, can miss the bound.
Values may be sent and summed in bfloat16 or wider, within the bound.
A program may use at most 128 MiB of HBM per device.

v0:
```python
import jax
import jax.numpy as jnp
from jax import lax
from jax.sharding import PartitionSpec as P

SLAB = 2048
ridge = 4.0


def solve_small(matrix, rhs):
    order = matrix.shape[-1]
    for pivot in range(order):
        scale = 1.0 / matrix[..., pivot, pivot]
        row_mat = matrix[..., pivot, :] * scale[..., None]
        row_rhs = rhs[..., pivot, :] * scale[..., None]
        factor = matrix[..., :, pivot]
        matrix = matrix - factor[..., :, None] * row_mat[..., None, :]
        rhs = rhs - factor[..., :, None] * row_rhs[..., None, :]
        matrix = matrix.at[..., pivot, :].set(row_mat)
        rhs = rhs.at[..., pivot, :].set(row_rhs)
    return rhs


def own_reduced(design, arc_partials, arc_id, arc_weight):
    high = lax.Precision.HIGHEST
    slab_rows = design[:, :SLAB].astype(jnp.float32)
    partials = arc_partials[0]
    coupling = jnp.dot(partials, slab_rows, precision=high, preferred_element_type=jnp.float32)
    gram = jnp.dot(partials, partials.T, precision=high, preferred_element_type=jnp.float32)
    arc_count = arc_weight.shape[0]
    select = (jnp.arange(arc_count) == arc_id[0]).astype(jnp.float32)
    arc_gram, arc_coupling = lax.psum(
        (select[:, None, None] * gram[None], select[:, None, None] * coupling[None]), ("row", "col")
    )
    order = partials.shape[0]
    own_gram = jnp.sum(select[:, None, None] * arc_gram, axis=0) + ridge * jnp.eye(
        order, dtype=jnp.float32
    )
    own_coupling = jnp.sum(select[:, None, None] * arc_coupling, axis=0)
    solved = solve_small(own_gram, own_coupling)
    reduced = slab_rows - jnp.dot(
        partials.T, solved, precision=high, preferred_element_type=jnp.float32
    )
    weight = jnp.sum(select * arc_weight)
    return (weight * reduced).astype(jnp.bfloat16)


def make_accumulate(ordered, piece):
    return lax.dot_general(
        piece, ordered, (((0,), (0,)), ((), ())), preferred_element_type=jnp.float32
    )


def col_major(slab_global, row_count, col_count, rows_dev):
    width = slab_global.shape[1]
    ordered = slab_global.reshape(row_count, col_count, rows_dev, width)
    return ordered.transpose(1, 0, 2, 3).reshape(rows_dev * row_count * col_count, width)


def local(design, arc_partials, arc_id, arc_weight):
    rows_dev = design.shape[0]
    row_count = lax.axis_size("row")
    col_count = lax.axis_size("col")
    devices = row_count * col_count
    epochs = rows_dev * devices
    eliminated_own = own_reduced(design, arc_partials, arc_id, arc_weight)
    regrouped = lax.all_to_all(design, "row", split_axis=1, concat_axis=0, tiled=True)
    columns = lax.all_to_all(eliminated_own, "col", split_axis=1, concat_axis=0, tiled=True)
    slab_global = lax.all_gather(columns, "row", axis=0, tiled=True)
    ordered = col_major(slab_global, row_count, col_count, rows_dev)
    normal = make_accumulate(ordered, lax.all_gather(regrouped, "col", axis=0, tiled=True))
    return normal * (1.0 / epochs)


def solution(mesh):
    placed = (P(("row", "col"), None), P(("row", "col"), None, None), P(("row", "col")), P())
    return jax.shard_map(
        local, mesh=mesh, in_specs=placed, out_specs=P("row", "col"), check_vma=False
    )
```

profile of v0, /device:TPU:0, one launch (start us, length us, event | category | flops | bytes accessed | tf_op | source)
XLA Modules:
  0.0 400.1 jit_solution(14108734418693655313)
XLA Ops:
  7.4 3.6 copy.42
  11.0 5.2 %all-to-all-start.1 = ((bf16[16,8,11264]{2,0,1:T(8,128)(2,1)}), bf16[16,8,11264]{2,0,1:T(8,128)(2,1)S(1)}, u32[]{:S(2)}, u32[]{:S(2)}) async-start(bf16[16,8,11264]{2,0,1:T(8,128)(2,1)} %bitcast.64), calls=%async_computation.1 | async-start | bytes 5767168 | tf_op jit(solution)/shard_map/all_to_all | solution.py:67
  16.9 1.0 fusion.3
  17.9 0.8 broadcast_multiply_fusion
  18.8 33.2 %all-to-all-done.1 = bf16[16,8,11264]{2,0,1:T(8,128)(2,1)S(1)} async-done(((bf16[16,8,11264]{2,0,1:T(8,128)(2,1)}), bf16[16,8,11264]{2,0,1:T(8,128)(2,1)S(1)}, u32[]{:S(2)}, u32[]{:S(2)}) %all-to-all-start.1) | async-done | bytes 2883616 | tf_op jit(solution)/shard_map/all_to_all | solution.py:67
  52.0 1.6 copy-done
  53.8 50.2 %psum.15 = f32[8,6,6]{2,0,1:T(8,128)S(1)} all-reduce(f32[8,6,6]{2,0,1:T(8,128)S(1)} %broadcast_multiply_fusion.1), channel_id=1, replica_groups=mesh['row'=8,'col'=4] {'row','col'}, use_global_device_ids=true, to_apply=%region_3.0 | all-reduce | flops 288 | bytes 2304 | tf_op jit(solution)/shard_map/psum | solution.py:32
  104.1 0.5 slice.240
  105.5 0.6 slice.244
  107.1 0.6 slice.248
  108.7 0.6 slice.252
  110.3 0.6 slice.256
  111.8 0.6 slice.260
  113.2 0.6 fusion.12
  114.0 216.3 %all-reduce.2.cloned.1.call-done = f32[8,6,2048]{2,0,1:T(8,128)} async-done(((f32[8,6,2048]{2,0,1:T(8,128)}), f32[8,6,2048]{2,0,1:T(8,128)}) %all-reduce.2.cloned.1.call-update) | async-done | bytes 393232 | tf_op jit(solution)/shard_map/psum | solution.py:32
  330.3 1.2 multiply_reduce_fusion
  331.6 0.2 scatter.36
  331.9 0.2 scatter.40
  332.1 0.2 scatter.44
  333.2 1.7 fusion.2
  334.9 9.2 %all_to_all.38 = bf16[16,4,512]{2,0,1:T(8,128)(2,1)S(1)} all-to-all(bf16[16,4,512]{2,0,1:T(8,128)(2,1)S(1)} %bitcast.70), channel_id=1, replica_groups=mesh['row'=8,'col'=4] {'col'}, dimensions={1} | all-to-all | bytes 131072 | tf_op jit(solution)/shard_map/all_to_all | solution.py:68
  344.1 9.8 %all_gather.6 = bf16[512,512]{1,0:T(8,128)(2,1)S(1)} all-gather(bf16[64,512]{1,0:T(8,128)(2,1)S(1)} %bitcast.69), channel_id=1, replica_groups=mesh['row'=8,'col'=4] {'row'}, dimensions={0}, use_global_device_ids=true | all-gather | bytes 589824 | tf_op jit(solution)/shard_map/all_gather | solution.py:69
  354.0 15.2 %multiply_bitcast_fusion = f32[11264,512]{0,1:T(8,128)} fusion(bf16[512,512]{1,0:T(8,128)(2,1)S(1)} %bitcast.65, bf16[512,11264]{1,0:T(8,128)(2,1)} %all-gather.2.cloned.1.call-done), kind=kOutput, calls=%fused_computation | convolution fusion | flops 5911347200 | bytes 35127296 | tf_op jit(solution)/shard_map/dot_general | solution.py:49
  369.1 23.5 %copy.24 = f32[11264,512]{1,0:T(8,128)} copy(f32[11264,512]{0,1:T(8,128)} %multiply_bitcast_fusion) | data formatting | bytes 46137344 | tf_op jit(solution)/shard_map/mul | solution.py:72
  (58 shorter events, 3.2 us)
Async XLA Ops:
  7.4 9.5 %copy-start.1 = (f32[1,6,16]{2,0,1:T(1,128)S(1)}, f32[1,6,16]{2,0,1:T(1,128)}, u32[]{:S(2)}) copy-start(f32[1,6,16]{2,0,1:T(1,128)} %param.27) | copy-start | bytes 1156
  7.4 105.8 %copy-start.2 = (f32[8]{0:T(128)S(1)}, f32[8]{0:T(128)}, u32[]{:S(2)}) copy-start(f32[8]{0:T(128)} %param.29) | copy-start | bytes 100
  11.0 41.0 %all-to-all-start.1 = ((bf16[16,8,11264]{2,0,1:T(8,128)(2,1)}), bf16[16,8,11264]{2,0,1:T(8,128)(2,1)S(1)}, u32[]{:S(2)}, u32[]{:S(2)}) async-start(bf16[16,8,11264]{2,0,1:T(8,128)(2,1)} %bitcast.64), calls=%async_computation.1 | async-start | bytes 5767168 | tf_op jit(solution)/shard_map/all_to_all | solution.py:67
  16.2 314.1 %all-reduce.2.cloned.1.call-start = ((), (), s32[]{:S(2)}) async-start(), calls=%async_computation.2 | async-start | bytes 786432 | tf_op jit(solution)/shard_map/psum | solution.py:32
  18.8 335.2 %all-gather.2.cloned.1.call-start = ((), (), s32[]{:S(2)}) async-start(), calls=%async_computation.3 | async-start | bytes 14417920 | tf_op jit(solution)/shard_map/all_gather | solution.py:71
  52.0 1.6 copy-start
Sparse Core Ops, SparseCore 0:
  22.3 307.9 all-reduce.1
Sparse Core Ops, SparseCore 1:
  53.7 201.6 all-gather.1
where the time goes:
time: 401 us; the launch traced here: 400 us
  waiting for transfers between devices  250 us (62%)
  blocking collectives  69.1 us (17%)
  local copies, waits for them, and re-layouts  34.6 us (9%)
  between operations  19.7 us (5%)
  matrix products  18 us (4%)
  starting transfers between devices  5.28 us (1%)
    psum x1, waiting for transfers between devices, own_reduced(): lax.psum((select[:, None, None] * gram[None], select[:, None, None] * cou...  216 us
    psum x1, blocking collectives, own_reduced(): lax.psum((select[:, None, None] * gram[None], select[:, None, None] * cou...  50.2 us
    all_to_all x1, waiting for transfers between devices, local(): lax.all_to_all(design, 'row', split_axis=1, concat_axis=0, tiled=True)  33.2 us
    mul x1, local copies, waits for them, and re-layouts, local(): return normal * (1.0 / epochs)  23.5 us
    dot_general x1, matrix products, make_accumulate(): lax.dot_general(piece, ordered, (((0,), (0,)), ((), ())), preferred_eleme...  15.2 us
    all_gather x1, blocking collectives, local(): slab_global = lax.all_gather(columns, 'row', axis=0, tiled=True)  9.79 us
    all_to_all x1, blocking collectives, local(): lax.all_to_all(eliminated_own, 'col', split_axis=1, concat_axis=0, tiled=...  9.18 us
  transfers between devices with their start and end apart: 3, of which 2 were waited for; matrix products, arithmetic and copies ran while one was open for 3% of the time, Pallas kernels for 0%

commit v1 on v0

--- a/solution.py
+++ b/solution.py
@@ -5,6 +5,29 @@
 
 SLAB = 2048
 ridge = 4.0
+
+
+def split_up(x, dim, size):
+    shape = x.shape
+    pieces = x.reshape(*shape[:dim], size, shape[dim] // size, *shape[dim + 1 :])
+    return jnp.moveaxis(pieces, dim, 0)
+
+
+def in_order(blocks, dim):
+    shape = list(blocks.shape[1:])
+    shape[dim] *= blocks.shape[0]
+    return jnp.moveaxis(blocks, 0, dim).reshape(shape)
+
+
+def exchange_in_pairs(x, axis, split_dim, concat_dim):
+    peers, here = (lax.axis_size(axis), lax.axis_index(axis))
+    tiles = split_up(x, split_dim, peers)
+    gathered = [tiles[here]]
+    for step in range(1, peers):
+        sent = tiles[here ^ step]
+        gathered.append(lax.ppermute(sent, axis, [(i, i ^ step) for i in range(peers)]))
+    tiles = jnp.stack(gathered)[here ^ jnp.arange(peers)]
+    return in_order(tiles, concat_dim)
 
 
 def solve_small(matrix, rhs):
@@ -64,7 +87,7 @@
     devices = row_count * col_count
     epochs = rows_dev * devices
     eliminated_own = own_reduced(design, arc_partials, arc_id, arc_weight)
-    regrouped = lax.all_to_all(design, "row", split_axis=1, concat_axis=0, tiled=True)
+    regrouped = exchange_in_pairs(design, "row", 1, 0)
     columns = lax.all_to_all(eliminated_own, "col", split_axis=1, concat_axis=0, tiled=True)
     slab_global = lax.all_gather(columns, "row", axis=0, tiled=True)
     ordered = col_major(slab_global, row_count, col_count, rows_dev)

time: 401 us -> 367 us (0.915)
  waiting for transfers between devices: 250 us -> 224 us
  local copies, waits for them, and re-layouts: 34.6 us -> 19.3 us
  starting transfers between devices: 5.28 us -> 9.67 us
    all_to_all x1 -> x0, waiting for transfers between devices: 33.2 us -> none  [local(): lax.all_to_all(design, 'row', split_axis=1, concat_axis=0, tiled=True)]
    ppermute x0 -> x7, waiting for transfers between devices: none -> 26.7 us  [exchange_in_pairs(): lax.ppermute(sent, axis, [(i, i ^ step) for i in range(peers)])]
    mul x1 -> x0, local copies, waits for them, and re-layouts: 23.5 us -> none  [local(): return normal * (1.0 / epochs)]
    psum x1, waiting for transfers between devices: 216 us -> 197 us  [own_reduced(): lax.psum((select[:, None, None] * gram[None], select[:, None, None] * cou...]
    ppermute x0 -> x7, starting transfers between devices: none -> 9.62 us  [exchange_in_pairs(): lax.ppermute(sent, axis, [(i, i ^ step) for i in range(peers)])]
    another operation x0 -> x2, local copies, waits for them, and re-layouts: none -> 6.04 us
    all_to_all x1 -> x0, starting transfers between devices: 5.2 us -> none  [local(): lax.all_to_all(design, 'row', split_axis=1, concat_axis=0, tiled=True)]
  transfers between devices with their start and end apart: 3 -> 9, of which waited for: 2 -> 4; matrix products, arithmetic and copies ran while one was open for 3% -> 6% of each run, Pallas kernels for 0% -> 0%
where the time goes in v1:
time: 367 us; the launch traced here: 366 us
  waiting for transfers between devices  224 us (61%)
  blocking collectives  71.3 us (19%)
  between operations  19.7 us (5%)
  local copies, waits for them, and re-layouts  19.3 us (5%)
  matrix products  18.7 us (5%)
  starting transfers between devices  9.67 us (3%)
  other arithmetic  3.81 us (1%)
    psum x1, waiting for transfers between devices, own_reduced(): lax.psum((select[:, None, None] * gram[None], select[:, None, None] * cou...  197 us
    psum x1, blocking collectives, own_reduced(): lax.psum((select[:, None, None] * gram[None], select[:, None, None] * cou...  52.1 us
    ppermute x7, waiting for transfers between devices, exchange_in_pairs(): lax.ppermute(sent, axis, [(i, i ^ step) for i in range(peers)])  26.7 us
    dot_general x1, matrix products, make_accumulate(): lax.dot_general(piece, ordered, (((0,), (0,)), ((), ())), preferred_eleme...  15.8 us
    all_gather x1, blocking collectives, local(): slab_global = lax.all_gather(columns, 'row', axis=0, tiled=True)  9.97 us
    ppermute x7, starting transfers between devices, exchange_in_pairs(): lax.ppermute(sent, axis, [(i, i ^ step) for i in range(peers)])  9.62 us
    all_to_all x1, blocking collectives, local(): lax.all_to_all(eliminated_own, 'col', split_axis=1, concat_axis=0, tiled=...  9.17 us
  transfers between devices with their start and end apart: 9, of which 4 were waited for; matrix products, arithmetic and copies ran while one was open for 6% of the time, Pallas kernels for 0%

profile of v1, /device:TPU:0, one launch (start us, length us, event | category | flops | bytes accessed | tf_op | source)
XLA Modules:
  0.0 366.1 jit_solution(3693378632902118710)
XLA Ops:
  8.0 1.0 fusion.3
  9.1 0.9 broadcast_multiply_fusion
  10.0 3.4 copy.23
  13.5 6.0 %constant_dynamic-slice_fusion = (bf16[16,1,11264]{2,1,0:T(2,128)(2,1)S(1)}, bf16[16,1,11264]{2,1,0:T(2,128)(2,1)S(1)}, bf16[16,1,11264]{2,1,0:T(2,128)(2,1)S(1)...) fusion(bf16[16,8,11264]{2,1,0:T(8,128)(2,1)S(1)} %bitcast.96, ...), kind=kLoop, calls=%fused_computation.62 | loop fusion | bytes 5767200 | tf_op jit(solution)/shard_map/dynamic-slice.73
  20.3 2.6 collective-permute-start.1
  23.3 1.8 collective-permute-start.3
  25.7 2.6 collective-permute-start.5
  28.4 4.1 %collective-permute-done.1 = bf16[16,11264]{1,0:T(8,128)(2,1)S(1)} collective-permute-done((bf16[16,11264]{1,0:T(8,128)(2,1)S(1)}, bf16[16,11264]{1,0:T(8,128)(2,1)S(1)}, u32[]{:S(2)}, u32[]{:S(2)}) %collective-permute-start.1) | collective-permute-done | bytes 360480 | tf_op jit(solution)/shard_map/ppermute | solution.py:28
  32.4 1.8 collective-permute-start.6
  34.3 5.8 %collective-permute-done.2 = bf16[16,11264]{1,0:T(8,128)(2,1)S(1)} collective-permute-done((bf16[16,11264]{1,0:T(8,128)(2,1)S(1)}, bf16[16,11264]{1,0:T(8,128)(2,1)S(1)}, u32[]{:S(2)}, u32[]{:S(2)}) %collective-permute-start.2) | collective-permute-done | bytes 360480 | tf_op jit(solution)/shard_map/ppermute | solution.py:28
  40.2 16.8 %collective-permute-done.4 = bf16[16,11264]{1,0:T(8,128)(2,1)S(1)} collective-permute-done((bf16[16,11264]{1,0:T(8,128)(2,1)S(1)}, bf16[16,11264]{1,0:T(8,128)(2,1)S(1)}, u32[]{:S(2)}, u32[]{:S(2)}) %collective-permute-start.4) | collective-permute-done | bytes 360480 | tf_op jit(solution)/shard_map/ppermute | solution.py:28
  57.1 2.3 gather_fusion
  59.5 0.7 copy-done
  60.3 52.1 %psum.15 = f32[8,6,6]{2,0,1:T(8,128)S(1)} all-reduce(f32[8,6,6]{2,0,1:T(8,128)S(1)} %broadcast_multiply_fusion.1), channel_id=1, replica_groups=mesh['row'=8,'col'=4] {'row','col'}, use_global_device_ids=true, to_apply=%region_3.0 | all-reduce | flops 288 | bytes 2304 | tf_op jit(solution)/shard_map/psum | solution.py:55
  113.9 0.6 slice.244
  115.4 0.6 slice.248
  118.5 0.6 slice.256
  121.3 0.7 fusion.12
  122.1 196.8 %all-reduce.2.cloned.1.call-done = f32[8,6,2048]{2,0,1:T(8,128)} async-done(((f32[8,6,2048]{2,0,1:T(8,128)}), f32[8,6,2048]{2,0,1:T(8,128)}) %all-reduce.2.cloned.1.call-update) | async-done | bytes 393232 | tf_op jit(solution)/shard_map/psum | solution.py:55
  318.9 1.2 multiply_reduce_fusion
  321.8 1.8 fusion.2
  323.7 9.2 %all_to_all.19 = bf16[16,4,512]{2,0,1:T(8,128)(2,1)S(1)} all-to-all(bf16[16,4,512]{2,0,1:T(8,128)(2,1)S(1)} %bitcast.110), channel_id=1, replica_groups=mesh['row'=8,'col'=4] {'col'}, dimensions={1} | all-to-all | bytes 131072 | tf_op jit(solution)/shard_map/all_to_all | solution.py:91
  332.9 10.0 %all_gather.7 = bf16[512,512]{1,0:T(8,128)(2,1)S(1)} all-gather(bf16[64,512]{1,0:T(8,128)(2,1)S(1)} %bitcast.109), channel_id=1, replica_groups=mesh['row'=8,'col'=4] {'row'}, dimensions={0}, use_global_device_ids=true | all-gather | bytes 589824 | tf_op jit(solution)/shard_map/all_gather | solution.py:92
  342.9 15.8 %convolution_multiply_fusion = f32[11264,512]{1,0:T(8,128)} fusion(bf16[512,11264]{1,0:T(8,128)(2,1)} %all-gather.2.cloned.1.call-done, bf16[512,512]{1,0:T(8,128)(2,1)S(1)} %bitcast.100), kind=kOutput, calls=%fused_computation.1 | convolution fusion | flops 5911347200 | bytes 35127296 | tf_op jit(solution)/shard_map/dot_general | solution.py:72
  (86 shorter events, 7.3 us)
Async XLA Ops:
  7.4 311.6 %all-reduce.2.cloned.1.call-start = ((), (), s32[]{:S(2)}) async-start(), calls=%async_computation.2 | async-start | bytes 786432 | tf_op jit(solution)/shard_map/psum | solution.py:55
  9.9 333.0 %all-gather.2.cloned.1.call-start = ((), (), s32[]{:S(2)}) async-start(), calls=%async_computation.1 | async-start | bytes 14417920 | tf_op jit(solution)/shard_map/all_gather | solution.py:94
  19.6 6.1 %collective-permute-start = (bf16[16,11264]{1,0:T(8,128)(2,1)S(1)}, bf16[16,11264]{1,0:T(8,128)(2,1)S(1)}, u32[]{:S(2)}, u32[]{:S(2)}) collective-permute-start(bf16[16,11264]{1,0:T(8,128)(2,1)S(1)} %bitcast.107), channel_id=1, source_target_pairs={{0,4},{4,0},{8,12},{12,8},{16,20},{20,16},{24,28},{28,24},{1,5},{5... | collective-permute-start | bytes 1081352 | tf_op jit(solution)/shard_map/ppermute | solution.py:28
  20.3 12.2 %collective-permute-start.1 = (bf16[16,11264]{1,0:T(8,128)(2,1)S(1)}, bf16[16,11264]{1,0:T(8,128)(2,1)S(1)}, u32[]{:S(2)}, u32[]{:S(2)}) collective-permute-start(bf16[16,11264]{1,0:T(8,128)(2,1)S(1)} %bitcast.106), channel_id=1, source_target_pairs={{0,8},{4,12},{8,0},{12,4},{16,24},{20,28},{24,16},{28,20},{1,9},{5... | collective-permute-start | bytes 1081352 | tf_op jit(solution)/shard_map/ppermute | solution.py:28
  23.0 17.1 %collective-permute-start.2 = (bf16[16,11264]{1,0:T(8,128)(2,1)S(1)}, bf16[16,11264]{1,0:T(8,128)(2,1)S(1)}, u32[]{:S(2)}, u32[]{:S(2)}) collective-permute-start(bf16[16,11264]{1,0:T(8,128)(2,1)S(1)} %bitcast.104), channel_id=1, source_target_pairs={{0,12},{4,8},{8,4},{12,0},{16,28},{20,24},{24,20},{28,16},{1,13},{... | collective-permute-start | bytes 1081352 | tf_op jit(solution)/shard_map/ppermute | solution.py:28
  23.3 16.9 %collective-permute-start.3 = (bf16[16,11264]{1,0:T(8,128)(2,1)S(1)}, bf16[16,11264]{1,0:T(8,128)(2,1)S(1)}, u32[]{:S(2)}, u32[]{:S(2)}) collective-permute-start(bf16[16,11264]{1,0:T(8,128)(2,1)S(1)} %bitcast.103), channel_id=1, source_target_pairs={{0,16},{4,20},{8,24},{12,28},{16,0},{20,4},{24,8},{28,12},{1,17},{... | collective-permute-start | bytes 1081352 | tf_op jit(solution)/shard_map/ppermute | solution.py:28
  25.2 31.8 %collective-permute-start.4 = (bf16[16,11264]{1,0:T(8,128)(2,1)S(1)}, bf16[16,11264]{1,0:T(8,128)(2,1)S(1)}, u32[]{:S(2)}, u32[]{:S(2)}) collective-permute-start(bf16[16,11264]{1,0:T(8,128)(2,1)S(1)} %bitcast.102), channel_id=1, source_target_pairs={{0,20},{4,16},{8,28},{12,24},{16,4},{20,0},{24,12},{28,8},{1,21},{... | collective-permute-start | bytes 1081352 | tf_op jit(solution)/shard_map/ppermute | solution.py:28
  25.7 31.3 %collective-permute-start.5 = (bf16[16,11264]{1,0:T(8,128)(2,1)S(1)}, bf16[16,11264]{1,0:T(8,128)(2,1)S(1)}, u32[]{:S(2)}, u32[]{:S(2)}) collective-permute-start(bf16[16,11264]{1,0:T(8,128)(2,1)S(1)} %bitcast.105), channel_id=1, source_target_pairs={{0,24},{4,28},{8,16},{12,20},{16,8},{20,12},{24,0},{28,4},{1,25},{... | collective-permute-start | bytes 1081352 | tf_op jit(solution)/shard_map/ppermute | solution.py:28
  32.4 24.6 %collective-permute-start.6 = (bf16[16,11264]{1,0:T(8,128)(2,1)S(1)}, bf16[16,11264]{1,0:T(8,128)(2,1)S(1)}, u32[]{:S(2)}, u32[]{:S(2)}) collective-permute-start(bf16[16,11264]{1,0:T(8,128)(2,1)S(1)} %bitcast.101), channel_id=1, source_target_pairs={{0,28},{4,24},{8,20},{12,16},{16,12},{20,8},{24,4},{28,0},{1,29},{... | collective-permute-start | bytes 1081352 | tf_op jit(solution)/shard_map/ppermute | solution.py:28
  59.4 0.7 copy-start
  59.4 61.8 %copy-start.1 = (f32[8]{0:T(128)S(1)}, f32[8]{0:T(128)}, u32[]{:S(2)}) copy-start(f32[8]{0:T(128)} %param.29) | copy-start | bytes 100
Sparse Core Ops, SparseCore 0:
  13.5 305.4 all-reduce.1
Sparse Core Ops, SparseCore 1:
  59.5 204.3 all-gather.1
